TPU v7x, 256 devices: a whole 4x4x8 slice. The times are simulated.
256 devices in a mesh: prime: 8 (over z), row: 32 (over x, y, core).
Axes of the slice: x: 4, y: 4, z: 8, core: 2. Of those that a mesh axis runs over, the one named last changes fastest.
Arguments:
- tile_data: bfloat16 [8, 128, 17, 128, 128], P('prime', 'row'), may hold values from -0.125 to 0.125
- tile_slots: int32 [8, 128, 17], P('prime', 'row'), may hold values from 0 to 67, as said below
- requests: int32 [8, 32, 32, 2], P('prime'), may hold values from 0 to 3, as said below
- start_panel: bfloat16 [8, 16384, 128], P('prime', 'row'), may hold values from -6 to 6
- projectors: bfloat16 [8, 16384, 128], P('prime', 'row'), may hold values from -0.09375 to 0.09375
- combine_weights: float32 [8, 8], replicated, may hold values from -2 to 2
Outputs:
- projections_mixed: float32 [8, 6, 128, 128], P(None, None, 'row', 'prime')
- final_panel: bfloat16 [8, 16384, 128], P('prime', 'row')
Inputs may be any that keep to these rules, and one draw needn't show every extreme that they name: `tile_slots`: for each system and each device of row, the last slot of each of its 4 block rows is 64 plus the row's index among them, and the other slots of its rows together name each of 0 to 63 exactly once. `requests`: for each system, taking device and source device, the 2 entries are different.
All inputs are finite; a program needn't handle non-finite values.
Results may differ from a plain program's by a relative error of at most 0.02.
Values may be sent and summed in bfloat16 or wider, within the bound.
A program may use at most 64 MiB of HBM per device.

v0:
```python
import jax
import jax.numpy as jnp
from jax import lax
from jax.sharding import PartitionSpec as P

ITERS = 6


def select_blocks(blocks, positions):
    return blocks[positions]


def shards(tile_data, tile_slots, requests, start_panel, projectors, combine_weights):
    rank_count = lax.axis_size("row")
    my_index = lax.axis_index("row")
    local_primes, local_blocks, stored_tiles, tile_rows, tile_cols = tile_data.shape
    vec_width = start_panel.shape[2]
    fetched = requests.shape[3]
    exchanged = rank_count * fetched
    pick_rows = jax.vmap(select_blocks)
    own_wants = lax.dynamic_index_in_dim(requests, my_index, 1, keepdims=False)
    flat_wants = own_wants.reshape(local_primes, exchanged)
    inside = jnp.clip(tile_slots, 0, exchanged - 1).reshape(local_primes, -1)
    picked = jnp.take_along_axis(flat_wants, inside, axis=1).reshape(tile_slots.shape)
    columns = jnp.where(
        tile_slots < exchanged,
        tile_slots // fetched * local_blocks + picked,
        my_index * local_blocks + tile_slots - exchanged,
    )
    current_panel = start_panel
    projections = []
    for iteration in range(ITERS):
        partial_sum = jnp.einsum(
            "prw,prv->pwv", projectors, current_panel, preferred_element_type=jnp.float32
        )
        projections.append(
            lax.psum_scatter(
                partial_sum.astype(jnp.bfloat16), "row", scatter_dimension=1, tiled=True
            ).astype(jnp.float32)
        )
        gathered = lax.all_gather(current_panel, "row", axis=1, tiled=True)
        gathered = gathered.reshape(local_primes, rank_count * local_blocks, tile_rows, vec_width)
        needed_blocks = pick_rows(gathered, columns)
        product = jnp.einsum(
            "pikab,pikbw->piaw", tile_data, needed_blocks, preferred_element_type=jnp.float32
        )
        current_panel = product.astype(jnp.bfloat16).reshape(
            local_primes, local_blocks * tile_rows, vec_width
        )
    stacked = jnp.stack(projections, axis=1)
    regrouped = lax.all_to_all(stacked, "prime", split_axis=3, concat_axis=0, tiled=True)
    combined = jnp.einsum(
        "qp,pkab->qkab", combine_weights, regrouped, precision=lax.Precision.HIGHEST
    )
    return (combined, current_panel)


def solution(mesh):
    return jax.shard_map(
        shards,
        mesh=mesh,
        in_specs=(
            P("prime", "row", None, None, None),
            P("prime", "row", None),
            P("prime", None, None, None),
            P("prime", "row", None),
            P("prime", "row", None),
            P(),
        ),
        out_specs=(P(None, None, "row", "prime"), P("prime", "row", None)),
        check_vma=False,
    )
```

profile of v0, /device:TPU:1, one launch (start us, length us, event | category | flops | bytes accessed | tf_op | source)
XLA Modules:
  0.0 486.8 jit_solution(9364935634181028703)
XLA Ops:
  7.2 0.7 all-gather.7.cloned.1.call-update
  8.0 0.7 constant_dynamic-slice_fusion.6
  8.8 0.7 broadcast_clamp_fusion
  9.6 1.2 gather_fusion
  11.0 0.7 fusion.71
  11.8 54.1 %all-gather.7.cloned.1.call-done = bf16[1,16384,128]{2,1,0:T(8,128)(2,1)} async-done(((bf16[1,512,128]{2,1,0:T(8,128)(2,1)}), bf16[1,16384,128]{2,1,0:T(8,128)(2,1)}) %all-gather.7.cloned.1.call-update) | async-done | bytes 4194320 | tf_op jit(solution)/shard_map/all_gather | solution.py:41
  65.9 4.7 gather_fusion.1
  70.6 3.0 fusion.30
  73.7 50.6 %all-gather.9.cloned.1.call-done = bf16[1,16384,128]{2,1,0:T(8,128)(2,1)} async-done(((bf16[1,512,128]{2,1,0:T(8,128)(2,1)}), bf16[1,16384,128]{2,1,0:T(8,128)(2,1)}) %all-gather.9.cloned.1.call-update) | async-done | bytes 4194320 | tf_op jit(solution)/shard_map/all_gather | solution.py:41
  124.3 4.7 gather_fusion.2
  129.0 3.0 fusion.33
  132.1 50.6 %all-gather.11.cloned.1.call-done = bf16[1,16384,128]{2,1,0:T(8,128)(2,1)} async-done(((bf16[1,512,128]{2,1,0:T(8,128)(2,1)}), bf16[1,16384,128]{2,1,0:T(8,128)(2,1)}) %all-gather.11.cloned.1.call-update) | async-done | bytes 4194320 | tf_op jit(solution)/shard_map/all_gather | solution.py:41
  182.8 4.7 gather_fusion.3
  187.4 3.0 fusion.36
  190.5 50.6 %all-gather.13.cloned.1.call-done = bf16[1,16384,128]{2,1,0:T(8,128)(2,1)} async-done(((bf16[1,512,128]{2,1,0:T(8,128)(2,1)}), bf16[1,16384,128]{2,1,0:T(8,128)(2,1)}) %all-gather.13.cloned.1.call-update) | async-done | bytes 4194320 | tf_op jit(solution)/shard_map/all_gather | solution.py:41
  241.2 4.7 gather_fusion.4
  245.9 3.1 fusion.39
  249.0 0.8 fusion.48
  250.1 0.7 copy.32
  251.1 0.7 copy.33
  251.8 0.2 fusion.51
  252.0 0.7 copy.34
  252.7 1.1 fusion.52
  253.9 0.7 copy.35
  254.6 45.0 %all-gather.15.cloned.1.call-done = bf16[1,16384,128]{2,1,0:T(8,128)(2,1)} async-done(((bf16[1,512,128]{2,1,0:T(8,128)(2,1)}), bf16[1,16384,128]{2,1,0:T(8,128)(2,1)}) %all-gather.15.cloned.1.call-update) | async-done | bytes 4194320 | tf_op jit(solution)/shard_map/all_gather | solution.py:41
  299.6 4.7 gather_fusion.5
  304.3 2.4 fusion.42
  306.8 0.2 fusion.53
  307.0 0.7 copy.36
  307.8 0.7 all-gather.17.cloned.1.call-update
  308.5 0.6 dynamic-slice
  309.8 108.3 %all-reduce.9.cloned.1.call-done = (bf16[1,128,128]{2,1,0:T(8,128)(2,1)}, bf16[1,128,128]{2,1,0:T(8,128)(2,1)}, bf16[1,128,128]{2,1,0:T(8,128)(2,1)}, bf16[1,128...) async-done(((bf16[1,128,128]{2,1,0:T(8,128)(2,1)}, bf16[1,128,128]{2,1,0:T(8,128)(2,1)}, bf16[1,128,128]{2,1,0:T(8,128)(2,1)}, ...) | async-done | bytes 196624
  418.1 0.7 constant_dynamic-update-slice_fusion.5
  418.7 0.7 constant_dynamic-update-slice_fusion.4
  419.4 0.7 constant_dynamic-update-slice_fusion.3
  420.1 0.7 constant_dynamic-update-slice_fusion.2
  420.8 0.7 constant_dynamic-update-slice_fusion.1
  421.5 0.7 constant_dynamic-update-slice_fusion
  422.3 0.3 reshape.336
  422.6 13.1 %all_to_all.18 = f32[8,1,384]{2,1,0:T(1,128)S(1)} all-to-all(f32[8,1,384]{2,1,0:T(1,128)S(1)} %reshape.336), channel_id=1, replica_groups=mesh['prime'=8,'row'=32] {'prime'}, dimensions={0} | all-to-all | bytes 24576 | tf_op jit(solution)/shard_map/all_to_all | solution.py:51
  435.8 0.5 broadcast.164
  436.3 0.7 reduce
  437.0 0.3 reshape.337
  437.3 0.3 copy.47
  437.9 0.7 copy.39
  438.5 33.7 %all-gather.17.cloned.1.call-done = bf16[1,16384,128]{2,1,0:T(8,128)(2,1)} async-done(((bf16[1,512,128]{2,1,0:T(8,128)(2,1)}), bf16[1,16384,128]{2,1,0:T(8,128)(2,1)}) %all-gather.17.cloned.1.call-update) | async-done | bytes 4194320 | tf_op jit(solution)/shard_map/all_gather | solution.py:41
  472.2 4.7 gather_fusion.6
  476.9 3.0 fusion.45
  (43 shorter events, 1.7 us)
Async XLA Ops:
  7.2 63.5 %copy-start = (bf16[1,4,17,128,128]{4,3,2,1,0:T(8,128)(2,1)S(1)}, bf16[1,4,17,128,128]{4,3,2,1,0:T(8,128)(2,1)}, u32[]{:S(2)}) copy-start(bf16[1,4,17,128,128]{4,3,2,1,0:T(8,128)(2,1)} %param.6) | copy-start | bytes 6684676
  7.2 58.7 %all-gather.7.cloned.1.call-start = ((), (), s32[]{:S(2)}) async-start(), calls=%async_computation.1 | async-start | bytes 4325376 | tf_op jit(solution)/shard_map/all_gather | solution.py:41
  7.9 116.4 %all-gather.9.cloned.1.call-start = ((), (), s32[]{:S(2)}) async-start(), calls=%async_computation.2 | async-start | bytes 4325376 | tf_op jit(solution)/shard_map/all_gather | solution.py:41
  73.7 109.1 %all-gather.11.cloned.1.call-start = ((), (), s32[]{:S(2)}) async-start(), calls=%async_computation.3 | async-start | bytes 4325376 | tf_op jit(solution)/shard_map/all_gather | solution.py:41
  132.1 109.1 %all-gather.13.cloned.1.call-start = ((), (), s32[]{:S(2)}) async-start(), calls=%async_computation.4 | async-start | bytes 4325376 | tf_op jit(solution)/shard_map/all_gather | solution.py:41
  190.5 109.2 %all-gather.15.cloned.1.call-start = ((), (), s32[]{:S(2)}) async-start(), calls=%async_computation.5 | async-start | bytes 4325376 | tf_op jit(solution)/shard_map/all_gather | solution.py:41
  245.8 3.2 copy-start.1
  245.8 3.2 copy-start.6
  245.8 4.1 copy-start.3
  245.8 5.0 %copy-start.4 = (bf16[4,128,128]{1,2,0:T(8,128)(2,1)S(1)}, bf16[4,128,128]{1,2,0:T(8,128)(2,1)}, u32[]{:S(2)}) copy-start(bf16[4,128,128]{1,2,0:T(8,128)(2,1)} %fusion.33) | copy-start | bytes 393220
  245.8 6.0 %copy-start.5 = (bf16[4,128,128]{1,2,0:T(8,128)(2,1)S(1)}, bf16[4,128,128]{1,2,0:T(8,128)(2,1)}, u32[]{:S(2)}) copy-start(bf16[4,128,128]{1,2,0:T(8,128)(2,1)} %fusion.36) | copy-start | bytes 393220
  249.0 169.1 %all-reduce.9.cloned.1.call-start = ((), (), s32[]{:S(2)}) async-start(), calls=%async_computation.7 | async-start | bytes 393216
  304.3 4.2 copy-start.8
  304.3 133.3 %copy-start.7 = (f32[8,8]{1,0:T(8,128)S(1)}, f32[8,8]{1,0:T(8,128)}, u32[]{:S(2)}) copy-start(f32[8,8]{1,0:T(8,128)} %param.11) | copy-start | bytes 772
  306.7 1.1 copy-start.2
  307.7 164.5 %all-gather.17.cloned.1.call-start = ((), (), s32[]{:S(2)}) async-start(), calls=%async_computation.6 | async-start | bytes 4325376 | tf_op jit(solution)/shard_map/all_gather | solution.py:41
Sparse Core Ops, SparseCore 0:
  10.6 55.2 all-gather.6
  73.8 50.5 all-gather.8
  132.2 50.5 all-gather.10
  190.6 50.5 all-gather.12
  249.1 50.5 all-gather.14
  307.9 110.1 all-reduce.8
  421.5 50.6 all-gather.16
where the time goes:
time: 488 us; the launch traced here: 487 us
  waiting for transfers between devices  394 us (81%)
  local copies, waits for them, and re-layouts  41.2 us (8%)
  matrix products  20.6 us (4%)
  between operations  14.9 us (3%)
  blocking collectives  13.1 us (3%)
    all_gather x6, waiting for transfers between devices, shards(): gathered = lax.all_gather(current_panel, 'row', axis=1, tiled=True)  285 us
    unnamed x8, waiting for transfers between devices  110 us
    gather x8, local copies, waits for them, and re-layouts, select_blocks(): return blocks[positions]  28.3 us
    dot_general x6, matrix products, shards(): jnp.einsum('pikab,pikbw->piaw', tile_data, needed_blocks, preferred_eleme...  17.5 us
    all_to_all x1, blocking collectives, shards(): lax.all_to_all(stacked, 'prime', split_axis=3, concat_axis=0, tiled=True)  13.1 us
  transfers between devices with their start and end apart: 7, of which 7 were waited for; matrix products, arithmetic and copies ran while one was open for 4% of the time, Pallas kernels for 0%

commit v1 on v0

v1 whole, which is shorter than its diff:
```python
import functools

import jax
import jax.numpy as jnp
import numpy as np
from jax import lax
from jax.experimental import pallas as pl
from jax.experimental.pallas import tpu as pltpu
from jax.sharding import PartitionSpec as P

ITERS = 6
TB = 128
MESH = pl.DeviceIdType.MESH

PLACES = (
    (0, 0),
    (3, 0), (1, 0), (0, 3), (0, 1),
    (2, 0), (0, 2), (3, 3), (3, 1), (1, 3), (1, 1),
    (2, 3), (2, 1), (3, 2), (1, 2),
    (2, 2),
)
SLOT = {place: at for at, place in enumerate(PLACES)}
NEAR = 16
ROWS = 512
HALF = 256
EXT = 528


def kernel(meta_ref, weights_ref, tiles_hbm, start_hbm, proj_hbm, mixed_ref, final_ref,
           panel, dense, tiles, proj, spread, columns, acc, terms, others,
           load_sem, prim_send, prim_fwd_send, sec_send, sec_fwd_send, sib_send,
           near_recv, sib_recv, col_send, col_recv, term_send, term_recv):
    z = lax.axis_index("prime")
    r = lax.axis_index("row")
    c = lax.rem(r, 2)
    y = lax.rem(r // 2, 4)
    x = r // 8

    def row_at(da, db):
        x_at = lax.rem(x + da * (1 - c) + db * c, 4)
        y_at = lax.rem(y + da * c + db * (1 - c), 4)
        return (x_at * 4 + y_at) * 2 + c

    a_up, a_down = (z, row_at(1, 0)), (z, row_at(3, 0))
    b_up, b_down = (z, row_at(0, 1)), (z, row_at(0, 3))
    sibling = (z, r + 1 - 2 * c)

    barrier = pltpu.get_barrier_semaphore()

    @pl.loop(1, 32)
    def _(d):
        pl.semaphore_signal(barrier, inc=1, device_id=(z, lax.rem(r + d, 32)), device_id_type=MESH)

    @pl.loop(1, 8)
    def _(d):
        pl.semaphore_signal(barrier, inc=1, device_id=(lax.rem(z + d, 8), r), device_id_type=MESH)

    load_proj = pltpu.make_async_copy(proj_hbm, proj, load_sem.at[0])
    load_start = pltpu.make_async_copy(start_hbm, panel.at[0, 0], load_sem.at[1])
    load_tiles = pltpu.make_async_copy(tiles_hbm, tiles, load_sem.at[2])
    load_proj.start()
    load_start.start()
    load_tiles.start()

    load_proj.wait()
    at_row = lax.broadcasted_iota(jnp.int32, (ROWS, ROWS), 0)
    at_col = lax.broadcasted_iota(jnp.int32, (ROWS, ROWS), 1)
    wanted = ((at_row >> 2) & 3) * TB + (at_row >> 4) * 4 + (at_row & 3)
    choose = jnp.where(at_col == wanted, 1.0, 0.0).astype(jnp.bfloat16)
    wide = jnp.concatenate([proj[pl.ds(q * TB, TB), :] for q in range(4)], axis=1)
    spread[...] = lax.dot_general(
        choose, wide, (((1,), (1,)), ((), ())), preferred_element_type=jnp.float32
    ).astype(jnp.bfloat16)

    pl.semaphore_wait(barrier, 38)

    def column_copy(d):
        to = lax.rem(r + d, 32)
        return pltpu.make_async_remote_copy(
            src_ref=spread.at[pl.ds(pl.multiple_of(to * 16, 16), 16)],
            dst_ref=columns.at[d],
            send_sem=col_send.at[d], recv_sem=col_recv.at[d],
            device_id=(z, to), device_id_type=MESH)

    @pl.loop(1, 32)
    def _(d):
        column_copy(d).start()

    columns[0] = spread[pl.ds(pl.multiple_of(r * 16, 16), 16), :]
    load_start.wait()
    load_tiles.wait()

    def build(slot):
        key = [meta_ref[64 + 2 * slot + which] for which in range(2)]
        tile = [tiles[meta_ref[2 * slot + which]] for which in range(2)]
        for i in range(4):
            for b in range(4):
                here = jnp.where(key[0] == i * 4 + b, tile[0],
                                 jnp.where(key[1] == i * 4 + b, tile[1], jnp.zeros_like(tile[1])))
                dense[slot, pl.ds(i * TB, TB), pl.ds(b * TB, TB)] = here
        part = columns[meta_ref[128 + slot]].astype(jnp.float32)
        band = lax.broadcasted_iota(jnp.int32, (16, TB), 0) >> 2
        for q in range(4):
            dense[slot, pl.ds(ROWS, 16), pl.ds(q * TB, TB)] = jnp.where(
                band == q, part, 0.0).astype(jnp.bfloat16)

    @pl.loop(0, ITERS)
    def _(t):
        par = lax.rem(t, 2)

        def piece(slot, h):
            return panel.at[par, slot, pl.ds(h * HALF, HALF)]

        def near(src, dst, h, send_sem, to):
            return pltpu.make_async_remote_copy(
                src_ref=piece(SLOT[src], h), dst_ref=piece(SLOT[dst], h),
                send_sem=send_sem, recv_sem=near_recv.at[par, SLOT[dst], h],
                device_id=to, device_id_type=MESH)

        prim = {}
        for h in range(2):
            prim[(3, 0), h] = near((0, 0), (3, 0), h, prim_send.at[0, h], a_up)
            prim[(1, 0), h] = near((0, 0), (1, 0), h, prim_send.at[1, h], a_down)
        prim[(2, 0), 0] = near((3, 0), (2, 0), 0, prim_fwd_send.at[0], a_up)
        prim[(2, 0), 1] = near((1, 0), (2, 0), 1, prim_fwd_send.at[1], a_down)
        sec = {}
        for k in range(4):
            for h in range(2):
                sec[(k, 3), h] = near((k, 0), (k, 3), h, sec_send.at[k, 0, h], b_up)
                sec[(k, 1), h] = near((k, 0), (k, 1), h, sec_send.at[k, 1, h], b_down)
            sec[(k, 2), 0] = near((k, 3), (k, 2), 0, sec_fwd_send.at[k, 0], b_up)
            sec[(k, 2), 1] = near((k, 1), (k, 2), 1, sec_fwd_send.at[k, 1], b_down)
        got = {**prim, **sec}
        sib = {}
        for place in PLACES:
            for h in range(2):
                sib[place, h] = pltpu.make_async_remote_copy(
                    src_ref=piece(SLOT[place], h), dst_ref=piece(NEAR + SLOT[place], h),
                    send_sem=sib_send.at[SLOT[place], h],
                    recv_sem=sib_recv.at[par, SLOT[place], h],
                    device_id=sibling, device_id_type=MESH)

        def pass_on(place, h):
            got[place, h].wait_recv()
            da, db = place
            if place == (3, 0) and h == 0:
                got[(2, 0), 0].start()
            if place == (1, 0) and h == 1:
                got[(2, 0), 1].start()
            if db == 0:
                first, second = ((da, 3), (da, 1)) if h == 0 else ((da, 1), (da, 3))
                got[first, h].start()
                got[second, h].start()
            if db == 3 and h == 0:
                got[(da, 2), 0].start()
            if db == 1 and h == 1:
                got[(da, 2), 1].start()
            sib[place, h].start()

        def add_up(low, high):
            def body(slot, carry):
                @pl.when(t == 0)
                def _():
                    build(slot)
                acc[...] += jnp.dot(dense[slot], panel[par, slot], preferred_element_type=jnp.float32)
                return carry
            lax.fori_loop(low, high, body, None)

        def take_sibling(places):
            for place in places:
                for h in range(2):
                    sib[place, h].wait_recv()

        prim[(3, 0), 0].start()
        prim[(1, 0), 1].start()
        prim[(3, 0), 1].start()
        prim[(1, 0), 0].start()
        sec[(0, 3), 0].start()
        sec[(0, 1), 1].start()
        sec[(0, 3), 1].start()
        sec[(0, 1), 0].start()
        for h in range(2):
            sib[(0, 0), h].start()

        for i in range(4):
            acc[pl.ds(i * TB, TB), :] = jnp.dot(
                tiles[i * 17 + 16], panel[par, 0, pl.ds(i * TB, TB), :],
                preferred_element_type=jnp.float32)
        acc[pl.ds(ROWS, 16), :] = jnp.zeros((16, TB), jnp.float32)

        @pl.when(t == 0)
        def _():
            @pl.loop(1, 32)
            def _(d):
                column_copy(d).wait()

        add_up(0, 1)
        one, two, three, four = PLACES[1:5], PLACES[5:11], PLACES[11:15], PLACES[15:]
        pass_on((3, 0), 0)
        pass_on((1, 0), 1)
        pass_on((3, 0), 1)
        pass_on((1, 0), 0)
        pass_on((0, 3), 0)
        pass_on((0, 1), 1)
        pass_on((0, 3), 1)
        pass_on((0, 1), 0)
        take_sibling(PLACES[:1])
        add_up(NEAR, NEAR + 1)
        pass_on((2, 0), 0)
        pass_on((2, 0), 1)
        add_up(1, 5)
        for place in two[1:]:
            for h in (0, 1):
                pass_on(place, h)
        take_sibling(one)
        add_up(NEAR + 1, NEAR + 5)
        add_up(5, 11)
        for place in three:
            for h in (0, 1):
                pass_on(place, h)
        take_sibling(two)
        add_up(NEAR + 5, NEAR + 11)
        add_up(11, 15)
        for h in (0, 1):
            pass_on((2, 2), h)
        take_sibling(three)
        add_up(NEAR + 11, NEAR + 15)
        add_up(15, 16)
        take_sibling(four)
        add_up(NEAR + 15, NEAR + 16)

        for copy in list(got.values()) + list(sib.values()):
            copy.wait_send()

        panel[1 - par, 0] = acc[pl.ds(0, ROWS), :].astype(jnp.bfloat16)
        low = acc[pl.ds(ROWS, 8), :] + acc[pl.ds(ROWS + 8, 8), :]
        terms[t] = low + pltpu.roll(low, 4, 0)

    def term_copy(d):
        return pltpu.make_async_remote_copy(
            src_ref=terms, dst_ref=others.at[d],
            send_sem=term_send.at[d], recv_sem=term_recv.at[d],
            device_id=(lax.rem(z + d, 8), r), device_id_type=MESH)

    for d in range(1, 8):
        term_copy(d).start()
    final_ref[...] = panel[ITERS % 2, 0]
    others[0] = terms[...]
    for d in range(1, 8):
        term_copy(d).wait()
    for q in range(8):
        total = jnp.zeros((ITERS, 8, TB), jnp.float32)
        for d in range(8):
            total += weights_ref[q, lax.rem(z + 8 - d, 8)] * others[d]
        mixed_ref[q] = total


def shards(tile_data, tile_slots, requests, start_panel, projectors, combine_weights):
    z = lax.axis_index("prime")
    r = lax.axis_index("row")
    c = r % 2
    y = (r // 2) % 4
    x = r // 8
    da = jnp.asarray(np.array([place[0] for place in PLACES] * 2, np.int32))
    db = jnp.asarray(np.array([place[1] for place in PLACES] * 2, np.int32))
    core = jnp.where(jnp.arange(32) < NEAR, c, 1 - c)
    x_at = (x + da * (1 - core) + db * core) % 4
    y_at = (y + da * core + db * (1 - core)) % 4
    source = (x_at * 4 + y_at) * 2 + core
    names = (source[:, None] * 2 + jnp.arange(2)[None, :]).reshape(64)
    flat_slots = tile_slots.reshape(68)
    spots = jnp.arange(68, dtype=jnp.int32)
    where_is = jnp.sum(jnp.where(flat_slots[None, :] == names[:, None], spots[None, :], 0), axis=1)
    own_wants = lax.dynamic_index_in_dim(requests, r, 1, keepdims=False).reshape(64)
    pick = jnp.sum(jnp.where(jnp.arange(64)[None, :] == names[:, None], own_wants[None, :], 0), axis=1)
    meta = jnp.concatenate([where_is, where_is // 17 * 4 + pick, (r - source + 32) % 32]).astype(jnp.int32)
    anywhere = pl.BlockSpec(memory_space=pl.ANY)
    small = pl.BlockSpec(memory_space=pltpu.SMEM)
    full = pl.BlockSpec(memory_space=pltpu.VMEM)
    dma = pltpu.SemaphoreType.DMA
    mixed, final = pl.pallas_call(
        kernel,
        out_shape=(
            jax.ShapeDtypeStruct((8, ITERS, 8, TB), jnp.float32),
            jax.ShapeDtypeStruct((ROWS, TB), jnp.bfloat16),
        ),
        in_specs=[small, small, anywhere, anywhere, anywhere],
        out_specs=(full, full),
        scratch_shapes=[
            pltpu.VMEM((2, 32, ROWS, TB), jnp.bfloat16),
            pltpu.VMEM((32, EXT, ROWS), jnp.bfloat16),
            pltpu.VMEM((68, TB, TB), jnp.bfloat16),
            pltpu.VMEM((ROWS, TB), jnp.bfloat16),
            pltpu.VMEM((ROWS, TB), jnp.bfloat16),
            pltpu.VMEM((32, 16, TB), jnp.bfloat16),
            pltpu.VMEM((EXT, TB), jnp.float32),
            pltpu.VMEM((ITERS, 8, TB), jnp.float32),
            pltpu.VMEM((8, ITERS, 8, TB), jnp.float32),
            dma((3,)), dma((2, 2)), dma((2,)), dma((4, 2, 2)), dma((4, 2)), dma((16, 2)),
            dma((2, 16, 2)), dma((2, 16, 2)), dma((32,)), dma((32,)), dma((8,)), dma((8,)),
        ],
        compiler_params=pltpu.CompilerParams(collective_id=0, has_side_effects=True),
    )(meta, combine_weights, tile_data.reshape(68, TB, TB), start_panel.reshape(ROWS, TB),
      projectors.reshape(ROWS, TB))
    mine = lax.dynamic_slice(mixed, (0, 0, 0, z * 16), (8, ITERS, 4, 16))
    return mine, final.reshape(1, ROWS, TB)


def solution(mesh):
    return jax.shard_map(
        shards,
        mesh=mesh,
        in_specs=(
            P("prime", "row", None, None, None),
            P("prime", "row", None),
            P("prime", None, None, None),
            P("prime", "row", None),
            P("prime", "row", None),
            P(),
        ),
        out_specs=(P(None, None, "row", "prime"), P("prime", "row", None)),
        check_vma=False,
    )
```

time: 488 us -> 155 us (0.32)
  waiting for transfers between devices: 394 us -> 0 us
  Pallas kernels: 0 us -> 147 us
  local copies, waits for them, and re-layouts: 41.2 us -> 4.34 us
  matrix products: 20.6 us -> 0 us
  between operations: 14.9 us -> 0.72 us
  blocking collectives: 13.1 us -> 0 us
    all_gather x6 -> x0, waiting for transfers between devices: 285 us -> none  [shards(): gathered = lax.all_gather(current_panel, 'row', axis=1, tiled=True)]
    pallas_call x0 -> x1, Pallas kernels: none -> 147 us  [shards(): pl.pallas_call(kernel, out_shape=(jax.ShapeDtypeStruct((8, ITERS, 8, TB),...]
    unnamed x8 -> x0, waiting for transfers between devices: 110 us -> none
    gather x10 -> x0, local copies, waits for them, and re-layouts: 29.6 us -> none  [the longest x8 28.3 us: select_blocks(): return blocks[positions]]
    dot_general x13 -> x0, matrix products: 20.6 us -> none  [the longest x6 17.5 us: shards(): jnp.einsum('pikab,pikbw->piaw', tile_data, needed_blocks, preferred_eleme...]
    all_to_all x1 -> x0, blocking collectives: 13.1 us -> none  [shards(): lax.all_to_all(stacked, 'prime', split_axis=3, concat_axis=0, tiled=True)]
  transfers between devices with their start and end apart: 7 -> 0, of which waited for: 7 -> 0; matrix products, arithmetic and copies ran while one was open for 4% -> 0% of each run, Pallas kernels for 0% -> 0%
where the time goes in v1:
time: 155 us; the launch traced here: 154 us
  Pallas kernels  147 us (95%)
  local copies, waits for them, and re-layouts  4.34 us (3%)
  other arithmetic  1.8 us (1%)
    pallas_call x1, Pallas kernels, shards(): pl.pallas_call(kernel, out_shape=(jax.ShapeDtypeStruct((8, ITERS, 8, TB),...  147 us

profile of v1, /device:TPU:1, one launch (start us, length us, event | category | flops | bytes accessed | tf_op | source)
XLA Modules:
  0.0 153.7 jit_solution(11746922468339329367)
XLA Ops:
  0.6 0.0 copy-start
  0.7 0.7 broadcast_multiply_fusion
  1.4 0.8 eq.35
  2.2 0.0 copy-done
  2.2 0.1 copy.12
  2.3 0.1 broadcast_in_dim.42
  2.4 0.1 iota_add_fusion
  2.4 0.1 add.99
  2.6 0.2 select_reduce_fusion.1
  2.7 0.2 select_reduce_fusion
  2.9 0.6 pad_add_fusion.meta_ref
  3.6 146.9 %shard_map.95 = (f32[8,6,8,128]{3,2,1,0:T(8,128)}, bf16[512,128]{1,0:T(8,128)(2,1)}) custom-call(s32[160]{0:T(256)} %pad_add_fusion.meta_ref, f32[8,8]{1,0:T(8,128)} %weights_ref.1, bf16[68,128,128]{2,1,0:T(8,128)(2,1)} %bitcast.6, bf16[512,128]{1,0:T(8,128)(2,1)} %bitcast.7, bf16[512,128]{1,0:T(8,128)(2,1)} %bitcast.8), custom_call_target="tpu_custom_call" | custom-call | tf_op jit(solution)/shard_map/pallas_call | solution.py:281
  150.5 1.7 %constant_dynamic-slice_fusion.1 = f32[8,6,4,16]{3,2,1,0:T(4,128)} fusion(f32[8,6,8,128]{3,2,1,0:T(8,128)} %get-tuple-element.4, s32[]{:T(128)S(6)} %select_n.68), kind=kLoop, calls=%fused_computation.24 | loop fusion | bytes 24580 | tf_op jit(solution)/shard_map/dynamic_slice | solution.py:305
  152.2 1.6 %copy.14 = bf16[1,512,128]{2,1,0:T(8,128)(2,1)} copy(bf16[1,512,128]{2,1,0:T(8,128)(2,1)} %bitcast.9) | data formatting | bytes 262144
  (3 shorter events, 0.0 us)
Async XLA Ops:
  0.6 1.5 %copy-start = (s32[1,32,32,2]{2,3,1,0:T(2,128)S(1)}, s32[1,32,32,2]{2,3,1,0:T(2,128)}, u32[]{:S(2)}) copy-start(s32[1,32,32,2]{2,3,1,0:T(2,128)} %param.10) | copy-start | bytes 24580

commit v2 on v1

--- a/solution.py
+++ b/solution.py
@@ -27,7 +27,7 @@
 
 
 def kernel(meta_ref, weights_ref, tiles_hbm, start_hbm, proj_hbm, mixed_ref, final_ref,
-           panel, dense, tiles, proj, spread, columns, acc, terms, others,
+           panel, bands, tiles, proj, spread, columns, acc, terms, others,
            load_sem, prim_send, prim_fwd_send, sec_send, sec_fwd_send, sib_send,
            near_recv, sib_recv, col_send, col_recv, term_send, term_recv):
     z = lax.axis_index("prime")
@@ -82,32 +82,24 @@
             send_sem=col_send.at[d], recv_sem=col_recv.at[d],
             device_id=(z, to), device_id_type=MESH)
 
-    @pl.loop(1, 32)
-    def _(d):
-        column_copy(d).start()
-
     columns[0] = spread[pl.ds(pl.multiple_of(r * 16, 16), 16), :]
     load_start.wait()
     load_tiles.wait()
 
     def build(slot):
-        key = [meta_ref[64 + 2 * slot + which] for which in range(2)]
-        tile = [tiles[meta_ref[2 * slot + which]] for which in range(2)]
-        for i in range(4):
-            for b in range(4):
-                here = jnp.where(key[0] == i * 4 + b, tile[0],
-                                 jnp.where(key[1] == i * 4 + b, tile[1], jnp.zeros_like(tile[1])))
-                dense[slot, pl.ds(i * TB, TB), pl.ds(b * TB, TB)] = here
         part = columns[meta_ref[128 + slot]].astype(jnp.float32)
         band = lax.broadcasted_iota(jnp.int32, (16, TB), 0) >> 2
         for q in range(4):
-            dense[slot, pl.ds(ROWS, 16), pl.ds(q * TB, TB)] = jnp.where(
+            bands[slot, :, pl.ds(q * TB, TB)] = jnp.where(
                 band == q, part, 0.0).astype(jnp.bfloat16)
 
-    @pl.loop(0, ITERS)
-    def _(t):
-        par = lax.rem(t, 2)
-
+    def term_copy(d, t):
+        return pltpu.make_async_remote_copy(
+            src_ref=terms.at[t], dst_ref=others.at[d, t],
+            send_sem=term_send.at[d, t], recv_sem=term_recv.at[d, t],
+            device_id=(lax.rem(z + d, 8), r), device_id_type=MESH)
+
+    def copies(par):
         def piece(slot, h):
             return panel.at[par, slot, pl.ds(h * HALF, HALF)]
 
@@ -117,28 +109,38 @@
                 send_sem=send_sem, recv_sem=near_recv.at[par, SLOT[dst], h],
                 device_id=to, device_id_type=MESH)
 
-        prim = {}
+        got = {}
         for h in range(2):
-            prim[(3, 0), h] = near((0, 0), (3, 0), h, prim_send.at[0, h], a_up)
-            prim[(1, 0), h] = near((0, 0), (1, 0), h, prim_send.at[1, h], a_down)
-        prim[(2, 0), 0] = near((3, 0), (2, 0), 0, prim_fwd_send.at[0], a_up)
-        prim[(2, 0), 1] = near((1, 0), (2, 0), 1, prim_fwd_send.at[1], a_down)
-        sec = {}
+            got[(3, 0), h] = near((0, 0), (3, 0), h, prim_send.at[par, 0, h], a_up)
+            got[(1, 0), h] = near((0, 0), (1, 0), h, prim_send.at[par, 1, h], a_down)
+        got[(2, 0), 0] = near((3, 0), (2, 0), 0, prim_fwd_send.at[par, 0], a_up)
+        got[(2, 0), 1] = near((1, 0), (2, 0), 1, prim_fwd_send.at[par, 1], a_down)
         for k in range(4):
             for h in range(2):
-                sec[(k, 3), h] = near((k, 0), (k, 3), h, sec_send.at[k, 0, h], b_up)
-                sec[(k, 1), h] = near((k, 0), (k, 1), h, sec_send.at[k, 1, h], b_down)
-            sec[(k, 2), 0] = near((k, 3), (k, 2), 0, sec_fwd_send.at[k, 0], b_up)
-            sec[(k, 2), 1] = near((k, 1), (k, 2), 1, sec_fwd_send.at[k, 1], b_down)
-        got = {**prim, **sec}
+                got[(k, 3), h] = near((k, 0), (k, 3), h, sec_send.at[par, k, 0, h], b_up)
+                got[(k, 1), h] = near((k, 0), (k, 1), h, sec_send.at[par, k, 1, h], b_down)
+            got[(k, 2), 0] = near((k, 3), (k, 2), 0, sec_fwd_send.at[par, k, 0], b_up)
+            got[(k, 2), 1] = near((k, 1), (k, 2), 1, sec_fwd_send.at[par, k, 1], b_down)
         sib = {}
         for place in PLACES:
             for h in range(2):
                 sib[place, h] = pltpu.make_async_remote_copy(
                     src_ref=piece(SLOT[place], h), dst_ref=piece(NEAR + SLOT[place], h),
-                    send_sem=sib_send.at[SLOT[place], h],
+                    send_sem=sib_send.at[par, SLOT[place], h],
                     recv_sem=sib_recv.at[par, SLOT[place], h],
                     device_id=sibling, device_id_type=MESH)
+        return got, sib
+
+    def finish_sends(par):
+        got, sib = copies(par)
+        for copy in list(got.values()) + list(sib.values()):
+            copy.wait_send()
+
+    @pl.loop(0, ITERS)
+    def _(t):
+        par = lax.rem(t, 2)
+
+        got, sib = copies(par)
 
         def pass_on(place, h):
             got[place, h].wait_recv()
@@ -157,30 +159,69 @@
                 got[(da, 2), 1].start()
             sib[place, h].start()
 
+        def products(slot):
+            parts = [panel[par, slot, pl.ds(b * TB, TB), :] for b in range(4)]
+            found = []
+            for which in range(2):
+                key = meta_ref[64 + 2 * slot + which]
+                pick = key & 3
+                block = jnp.where(pick == 0, parts[0], jnp.where(
+                    pick == 1, parts[1], jnp.where(pick == 2, parts[2], parts[3])))
+                found.append((key >> 2, jnp.dot(
+                    tiles[meta_ref[2 * slot + which]], block, preferred_element_type=jnp.float32)))
+            term = jnp.dot(bands[slot], panel[par, slot], preferred_element_type=jnp.float32)
+            return found, term
+
         def add_up(low, high):
-            def body(slot, carry):
+            step = 2 - (high - low) % 2
+
+            def body(at, carry):
+                slots = [low + at * step + n for n in range(step)]
+
                 @pl.when(t == 0)
                 def _():
-                    build(slot)
-                acc[...] += jnp.dot(dense[slot], panel[par, slot], preferred_element_type=jnp.float32)
+                    for slot in slots:
+                        build(slot)
+                found, term = [], None
+                for slot in slots:
+                    more, part = products(slot)
+                    found += more
+                    term = part if term is None else term + part
+                acc[pl.ds(ROWS, 16), :] += term
+                for i in range(4):
+                    total = acc[pl.ds(i * TB, TB), :]
+                    for row, product in found:
+                        total = total + jnp.where(row == i, product, 0.0)
+                    acc[pl.ds(i * TB, TB), :] = total
                 return carry
-            lax.fori_loop(low, high, body, None)
+            lax.fori_loop(0, (high - low) // step, body, None)
 
         def take_sibling(places):
             for place in places:
                 for h in range(2):
                     sib[place, h].wait_recv()
 
-        prim[(3, 0), 0].start()
-        prim[(1, 0), 1].start()
-        prim[(3, 0), 1].start()
-        prim[(1, 0), 0].start()
-        sec[(0, 3), 0].start()
-        sec[(0, 1), 1].start()
-        sec[(0, 3), 1].start()
-        sec[(0, 1), 0].start()
+        got[(3, 0), 0].start()
+        got[(1, 0), 1].start()
+        got[(3, 0), 1].start()
+        got[(1, 0), 0].start()
+        got[(0, 3), 0].start()
+        got[(0, 1), 1].start()
+        got[(0, 3), 1].start()
+        got[(0, 1), 0].start()
         for h in range(2):
             sib[(0, 0), h].start()
+
+        @pl.when(t == 0)
+        def _():
+            @pl.loop(1, 32)
+            def _(d):
+                column_copy(d).start()
+
+        @pl.when(t > 0)
+        def _():
+            for d in range(1, 8):
+                term_copy(d, t - 1).start()
 
         for i in range(4):
             acc[pl.ds(i * TB, TB), :] = jnp.dot(
@@ -195,6 +236,11 @@
                 column_copy(d).wait()
 
         add_up(0, 1)
+
+        @pl.when(t > 0)
+        def _():
+            finish_sends(1 - par)
+
         one, two, three, four = PLACES[1:5], PLACES[5:11], PLACES[11:15], PLACES[15:]
         pass_on((3, 0), 0)
         pass_on((1, 0), 1)
@@ -229,34 +275,29 @@
         take_sibling(four)
         add_up(NEAR + 15, NEAR + 16)
 
-        for copy in list(got.values()) + list(sib.values()):
-            copy.wait_send()
-
         panel[1 - par, 0] = acc[pl.ds(0, ROWS), :].astype(jnp.bfloat16)
         low = acc[pl.ds(ROWS, 8), :] + acc[pl.ds(ROWS + 8, 8), :]
         terms[t] = low + pltpu.roll(low, 4, 0)
 
-    def term_copy(d):
-        return pltpu.make_async_remote_copy(
-            src_ref=terms, dst_ref=others.at[d],
-            send_sem=term_send.at[d], recv_sem=term_recv.at[d],
-            device_id=(lax.rem(z + d, 8), r), device_id_type=MESH)
-
     for d in range(1, 8):
-        term_copy(d).start()
+        term_copy(d, ITERS - 1).start()
     final_ref[...] = panel[ITERS % 2, 0]
     others[0] = terms[...]
-    for d in range(1, 8):
-        term_copy(d).wait()
+    finish_sends((ITERS - 1) % 2)
+
+    @pl.loop(0, ITERS)
+    def _(t):
+        for d in range(1, 8):
+            term_copy(d, t).wait()
+    turn = lax.rem(TB - z * 16, TB)
     for q in range(8):
         total = jnp.zeros((ITERS, 8, TB), jnp.float32)
         for d in range(8):
             total += weights_ref[q, lax.rem(z + 8 - d, 8)] * others[d]
-        mixed_ref[q] = total
+        mixed_ref[q] = pltpu.roll(total, turn, 2)[:, :4, :16]
 
 
 def shards(tile_data, tile_slots, requests, start_panel, projectors, combine_weights):
-    z = lax.axis_index("prime")
     r = lax.axis_index("row")
     c = r % 2
     y = (r // 2) % 4
@@ -281,14 +322,14 @@
     mixed, final = pl.pallas_call(
         kernel,
         out_shape=(
-            jax.ShapeDtypeStruct((8, ITERS, 8, TB), jnp.float32),
+            jax.ShapeDtypeStruct((8, ITERS, 4, 16), jnp.float32),
             jax.ShapeDtypeStruct((ROWS, TB), jnp.bfloat16),
         ),
         in_specs=[small, small, anywhere, anywhere, anywhere],
         out_specs=(full, full),
         scratch_shapes=[
             pltpu.VMEM((2, 32, ROWS, TB), jnp.bfloat16),
-            pltpu.VMEM((32, EXT, ROWS), jnp.bfloat16),
+            pltpu.VMEM((32, 16, ROWS), jnp.bfloat16),
             pltpu.VMEM((68, TB, TB), jnp.bfloat16),
             pltpu.VMEM((ROWS, TB), jnp.bfloat16),
             pltpu.VMEM((ROWS, TB), jnp.bfloat16),
@@ -296,14 +337,13 @@
             pltpu.VMEM((EXT, TB), jnp.float32),
             pltpu.VMEM((ITERS, 8, TB), jnp.float32),
             pltpu.VMEM((8, ITERS, 8, TB), jnp.float32),
-            dma((3,)), dma((2, 2)), dma((2,)), dma((4, 2, 2)), dma((4, 2)), dma((16, 2)),
-            dma((2, 16, 2)), dma((2, 16, 2)), dma((32,)), dma((32,)), dma((8,)), dma((8,)),
+            dma((3,)), dma((2, 2, 2)), dma((2, 2)), dma((2, 4, 2, 2)), dma((2, 4, 2)), dma((2, 16, 2)),
+            dma((2, 16, 2)), dma((2, 16, 2)), dma((32,)), dma((32,)), dma((8, ITERS)), dma((8, ITERS)),
         ],
         compiler_params=pltpu.CompilerParams(collective_id=0, has_side_effects=True),
     )(meta, combine_weights, tile_data.reshape(68, TB, TB), start_panel.reshape(ROWS, TB),
       projectors.reshape(ROWS, TB))
-    mine = lax.dynamic_slice(mixed, (0, 0, 0, z * 16), (8, ITERS, 4, 16))
-    return mine, final.reshape(1, ROWS, TB)
+    return mixed, final.reshape(1, ROWS, TB)
 
 
 def solution(mesh):

time: 155 us -> 139 us (0.90)
  Pallas kernels: 147 us -> 132 us
    pallas_call x1, Pallas kernels: 147 us -> 132 us  [shards(): pl.pallas_call(kernel, out_shape=(jax.ShapeDtypeStruct((8, ITERS, 4, 16),...]
    dynamic_slice x1 -> x0, local copies, waits for them, and re-layouts: 1.69 us -> none  [shards(): mine = lax.dynamic_slice(mixed, (0, 0, 0, z * 16), (8, ITERS, 4, 16))]
    unnamed x3 -> x4, local copies, waits for them, and re-layouts: 1.58 us -> 3.12 us
where the time goes in v2:
time: 139 us
  Pallas kernels  132 us (95%)
  local copies, waits for them, and re-layouts  4.19 us (3%)
  other arithmetic  1.8 us (1%)
    pallas_call x1, Pallas kernels, shards(): pl.pallas_call(kernel, out_shape=(jax.ShapeDtypeStruct((8, ITERS, 4, 16),...  132 us
    unnamed x4, local copies, waits for them, and re-layouts  3.12 us

profile of v2, /device:TPU:1, one launch (start us, length us, event | category | flops | bytes accessed | tf_op | source)
XLA Modules:
  0.0 138.8 jit_solution(13093075167006755650)
XLA Ops:
  0.6 0.0 copy-start
  0.7 0.7 broadcast_multiply_fusion
  1.4 0.8 eq.35
  2.2 0.0 copy-done
  2.2 0.1 copy.12
  2.3 0.1 broadcast_in_dim.42
  2.4 0.1 iota_add_fusion
  2.4 0.1 add.96
  2.6 0.2 select_reduce_fusion.1
  2.7 0.2 select_reduce_fusion
  2.9 0.6 pad_add_fusion.meta_ref
  3.6 132.1 %shard_map.95 = (f32[8,6,4,16]{3,2,1,0:T(4,128)}, bf16[512,128]{1,0:T(8,128)(2,1)}) custom-call(s32[160]{0:T(256)} %pad_add_fusion.meta_ref, f32[8,8]{1,0:T(8,128)} %weights_ref.1, bf16[68,128,128]{2,1,0:T(8,128)(2,1)} %bitcast.6, bf16[512,128]{1,0:T(8,128)(2,1)} %bitcast.7, bf16[512,128]{1,0:T(8,128)(2,1)} %bitcast.8), custom_call_target="tpu_custom_call" | custom-call | tf_op jit(solution)/shard_map/pallas_call | solution.py:322
  135.7 1.5 %copy.15 = f32[8,6,4,16]{3,2,1,0:T(4,128)} copy(f32[8,6,4,16]{3,2,1,0:T(4,128)} %get-tuple-element.10) | data formatting | bytes 24576
  137.3 1.6 %copy.16 = bf16[1,512,128]{2,1,0:T(8,128)(2,1)} copy(bf16[1,512,128]{2,1,0:T(8,128)(2,1)} %bitcast.9) | data formatting | bytes 262144
  (3 shorter events, 0.0 us)
Async XLA Ops:
  0.6 1.5 %copy-start = (s32[1,32,32,2]{2,3,1,0:T(2,128)S(1)}, s32[1,32,32,2]{2,3,1,0:T(2,128)}, u32[]{:S(2)}) copy-start(s32[1,32,32,2]{2,3,1,0:T(2,128)} %param.10) | copy-start | bytes 24580

commit v3 on v2

--- a/solution.py
+++ b/solution.py
@@ -229,6 +229,14 @@
                 preferred_element_type=jnp.float32)
         acc[pl.ds(ROWS, 16), :] = jnp.zeros((16, TB), jnp.float32)
 
+        @pl.when(t > 0)
+        def _():
+            finish_sends(1 - par)
+
+        for place, h in (((3, 0), 0), ((1, 0), 1), ((0, 3), 0), ((0, 1), 1),
+                         ((3, 0), 1), ((1, 0), 0), ((0, 3), 1), ((0, 1), 0)):
+            pass_on(place, h)
+
         @pl.when(t == 0)
         def _():
             @pl.loop(1, 32)
@@ -236,43 +244,35 @@
                 column_copy(d).wait()
 
         add_up(0, 1)
-
-        @pl.when(t > 0)
-        def _():
-            finish_sends(1 - par)
-
-        one, two, three, four = PLACES[1:5], PLACES[5:11], PLACES[11:15], PLACES[15:]
-        pass_on((3, 0), 0)
-        pass_on((1, 0), 1)
-        pass_on((3, 0), 1)
-        pass_on((1, 0), 0)
-        pass_on((0, 3), 0)
-        pass_on((0, 1), 1)
-        pass_on((0, 3), 1)
-        pass_on((0, 1), 0)
         take_sibling(PLACES[:1])
         add_up(NEAR, NEAR + 1)
+        add_up(1, 5)
         pass_on((2, 0), 0)
         pass_on((2, 0), 1)
-        add_up(1, 5)
-        for place in two[1:]:
+        take_sibling(PLACES[1:5])
+        add_up(NEAR + 1, NEAR + 5)
+        pass_on((0, 2), 0)
+        pass_on((0, 2), 1)
+        for place, h in (((3, 3), 0), ((3, 1), 0), ((1, 1), 1), ((1, 3), 1),
+                         ((3, 3), 1), ((3, 1), 1), ((1, 1), 0), ((1, 3), 0)):
+            pass_on(place, h)
+        add_up(5, 9)
+        for place, h in (((2, 3), 0), ((2, 1), 1), ((2, 3), 1), ((2, 1), 0)):
+            pass_on(place, h)
+        add_up(9, 11)
+        take_sibling(PLACES[5:11])
+        add_up(NEAR + 5, NEAR + 9)
+        for place in PLACES[13:15]:
             for h in (0, 1):
                 pass_on(place, h)
-        take_sibling(one)
-        add_up(NEAR + 1, NEAR + 5)
-        add_up(5, 11)
-        for place in three:
-            for h in (0, 1):
-                pass_on(place, h)
-        take_sibling(two)
-        add_up(NEAR + 5, NEAR + 11)
+        add_up(NEAR + 9, NEAR + 11)
         add_up(11, 15)
         for h in (0, 1):
             pass_on((2, 2), h)
-        take_sibling(three)
+        take_sibling(PLACES[11:15])
         add_up(NEAR + 11, NEAR + 15)
         add_up(15, 16)
-        take_sibling(four)
+        take_sibling(PLACES[15:])
         add_up(NEAR + 15, NEAR + 16)
 
         panel[1 - par, 0] = acc[pl.ds(0, ROWS), :].astype(jnp.bfloat16)

time: 139 us -> 130 us (0.935)
  Pallas kernels: 132 us -> 123 us
    pallas_call x1, Pallas kernels: 132 us -> 123 us  [shards(): pl.pallas_call(kernel, out_shape=(jax.ShapeDtypeStruct((8, ITERS, 4, 16),...]
where the time goes in v3:
time: 130 us
  Pallas kernels  123 us (95%)
  local copies, waits for them, and re-layouts  4.19 us (3%)
  other arithmetic  1.8 us (1%)
    pallas_call x1, Pallas kernels, shards(): pl.pallas_call(kernel, out_shape=(jax.ShapeDtypeStruct((8, ITERS, 4, 16),...  123 us
    unnamed x4, local copies, waits for them, and re-layouts  3.12 us

profile of v3, /device:TPU:1, one launch (start us, length us, event | category | flops | bytes accessed | tf_op | source)
XLA Modules:
  0.0 129.6 jit_solution(2552749704158221815)
XLA Ops:
  0.6 0.0 copy-start
  0.7 0.7 broadcast_multiply_fusion
  1.4 0.8 eq.35
  2.2 0.0 copy-done
  2.2 0.1 copy.12
  2.3 0.1 broadcast_in_dim.42
  2.4 0.1 iota_add_fusion
  2.4 0.1 add.96
  2.6 0.2 select_reduce_fusion.1
  2.7 0.2 select_reduce_fusion
  2.9 0.6 pad_add_fusion.meta_ref
  3.6 122.9 %shard_map.95 = (f32[8,6,4,16]{3,2,1,0:T(4,128)}, bf16[512,128]{1,0:T(8,128)(2,1)}) custom-call(s32[160]{0:T(256)} %pad_add_fusion.meta_ref, f32[8,8]{1,0:T(8,128)} %weights_ref.1, bf16[68,128,128]{2,1,0:T(8,128)(2,1)} %bitcast.6, bf16[512,128]{1,0:T(8,128)(2,1)} %bitcast.7, bf16[512,128]{1,0:T(8,128)(2,1)} %bitcast.8), custom_call_target="tpu_custom_call" | custom-call | tf_op jit(solution)/shard_map/pallas_call | solution.py:322
  126.5 1.5 %copy.15 = f32[8,6,4,16]{3,2,1,0:T(4,128)} copy(f32[8,6,4,16]{3,2,1,0:T(4,128)} %get-tuple-element.10) | data formatting | bytes 24576
  128.1 1.6 %copy.16 = bf16[1,512,128]{2,1,0:T(8,128)(2,1)} copy(bf16[1,512,128]{2,1,0:T(8,128)(2,1)} %bitcast.9) | data formatting | bytes 262144
  (3 shorter events, 0.0 us)
Async XLA Ops:
  0.6 1.5 %copy-start = (s32[1,32,32,2]{2,3,1,0:T(2,128)S(1)}, s32[1,32,32,2]{2,3,1,0:T(2,128)}, u32[]{:S(2)}) copy-start(s32[1,32,32,2]{2,3,1,0:T(2,128)} %param.10) | copy-start | bytes 24580
